TPU v7x, 32 devices: a whole 2x2x4 slice. The times are simulated.
32 devices in a mesh: prow: 4 (over y, x), pcol: 8 (over z, core).
Axes of the slice: x: 2, y: 2, z: 4, core: 2. Of those that a mesh axis runs over, the one named last changes fastest.
Arguments:
- rhs: bfloat16 [3, 8, 512, 128], P(None, 'pcol', 'prow'), may hold values from -6 to 6
- inverse_diagonal_blocks: bfloat16 [3, 8, 512, 512], P(None, 'pcol'), may hold values from -1 to 2, as said below
- offdiagonal_blocks: bfloat16 [2, 8, 4, 512, 512], P(None, 'pcol', 'prow'), may hold values from -0.09375 to 0.09375
- targets: int32 [2, 8, 4], P(None, 'pcol'), may hold values from 0 to 15, as said below
Outputs:
- solution: bfloat16 [3, 8, 512, 128], P(None, 'pcol', 'prow')
Inputs may be any that keep to these rules, and one draw needn't show every extreme that they name: For a supernode of level l the 4 entries of targets[l] are distinct and lie between l * 8 and (2) * 8 - 1, so they name supernodes of later levels only. Each block of inverse_diagonal_blocks is lower triangular.
All inputs are finite; a program needn't handle non-finite values.
Results may differ from a plain program's by a relative error of at most 0.014.
Values may be sent and summed in bfloat16 or wider, within the bound.
No kernel may reach another device: no remote copies, remote signals or barrier semaphores. Data moves between devices by JAX's collectives and lax.ppermute only.
A program may use at most 64 MiB of HBM per device.

v0:
```python
import jax
import jax.numpy as jnp
from jax import lax
from jax.sharding import PartitionSpec as P


def local(rhs, inverse_diagonal_blocks, offdiagonal_blocks, targets):
    levels = rhs.shape[0]
    per_group = rhs.shape[1]
    part_rows = rhs.shape[2]
    vector_count = rhs.shape[3]
    per_device = offdiagonal_blocks.shape[2]
    row_count = lax.axis_size("prow")
    level_size = per_group * lax.axis_size("pcol")
    upper_count = levels - 1
    row_index = lax.axis_index("prow")
    gathered_updates = jnp.zeros(
        (upper_count, row_count, level_size, part_rows, vector_count), jnp.float32
    )
    outputs = []
    for present_level in range(levels):
        remaining_rhs = rhs[present_level].astype(jnp.float32)
        if present_level > 0:
            due_block = gathered_updates[present_level - 1]
            reduced_once = lax.psum_scatter(
                due_block.astype(jnp.bfloat16), "pcol", scatter_dimension=1, tiled=True
            )
            arrived = lax.psum_scatter(
                reduced_once, "prow", scatter_dimension=0, tiled=True
            ).astype(jnp.float32)[0]
            remaining_rhs = remaining_rhs - arrived
        whole_block = lax.all_gather(remaining_rhs, "prow", axis=1, tiled=True)
        finished_unknowns = jnp.einsum(
            "rqe,rei->rqi",
            inverse_diagonal_blocks[present_level].astype(jnp.float32),
            whole_block,
            precision=lax.Precision.HIGHEST,
        ).astype(jnp.bfloat16)
        supernode_rows = lax.dynamic_slice_in_dim(
            finished_unknowns, row_index * part_rows, part_rows, 1
        )
        outputs.append(supernode_rows)
        if present_level < upper_count:
            products = jnp.einsum(
                "wsiq,wqm->wsim",
                offdiagonal_blocks[present_level],
                finished_unknowns,
                preferred_element_type=jnp.float32,
            )
            chosen = lax.dynamic_slice_in_dim(
                targets[present_level], row_index * per_device, per_device, 1
            )
            chosen = chosen.reshape(per_group * per_device)
            level_ids = chosen // level_size
            node_ids = chosen % level_size
            moved_rows = products.reshape(
                per_group * per_device, row_count, part_rows, vector_count
            )
            gathered_updates = gathered_updates.at[level_ids, :, node_ids].add(moved_rows)
    return jnp.stack(outputs)


def solution(mesh):
    in_specs = (
        P(None, "pcol", "prow", None),
        P(None, "pcol", None, None),
        P(None, "pcol", "prow", None, None),
        P(None, "pcol", None),
    )
    out_specs = P(None, "pcol", "prow", None)
    return jax.shard_map(local, mesh=mesh, in_specs=in_specs, out_specs=out_specs, check_vma=False)
```

profile of v0, /device:TPU:0, one launch (start us, length us, event | category | flops | bytes accessed | tf_op | source)
XLA Modules:
  0.0 184.7 jit_solution(10603757281627997184)
XLA Ops:
  6.5 0.0 reduce-scatter.15.cloned.1.call-start
  6.5 0.7 fusion.22
  7.2 0.6 constant_dynamic-slice_fusion
  13.0 0.8 fusion.21
  13.8 10.5 %all-gather = f32[1,1,512,128]{3,2,1,0:T(8,128)S(1)} all-gather(f32[1,1,128,128]{3,2,1,0:T(8,128)S(1)} %get-tuple-element.35), channel_id=2, replica_groups=mesh['prow'=4,'pcol'=8] {'prow'}, dimensions={2}, use_global_device_ids=true | all-gather | bytes 327680 | tf_op jit(solution)/shard_map/all_gather | solution.py:32
  24.3 1.3 fusion.20
  25.6 0.1 concatenate.10
  25.7 0.1 concatenate.11
  25.7 1.6 convolution_convert_fusion.1
  27.4 1.4 and_reduce_fusion
  28.7 0.0 copy-start.1
  28.7 0.5 broadcast_in_dim.2
  29.2 0.9 fusion.1
  30.2 0.0 copy-start
  30.2 1.9 %copy-done = f32[2,4,8,128,128]{3,4,1,2,0:T(8,128)} copy-done((f32[2,4,8,128,128]{3,4,1,2,0:T(8,128)}, f32[2,4,8,128,128]{3,4,1,2,0:T(8,128)S(1)}, u32[]{:S(2)}) %copy-start) | copy-done | bytes 4194328
  32.1 1.1 fusion.5
  33.3 0.0 reduce-scatter.15.cloned.1.call-update
  33.3 0.0 reduce-scatter.19.cloned.1.call-start
  33.3 33.0 %reduce-scatter.15.cloned.1.call-done = bf16[4,1,128,128]{2,3,0,1:T(8,128)(2,1)} async-done(((bf16[4,8,128,128]{2,3,0,1:T(8,128)(2,1)}), bf16[4,1,128,128]{2,3,0,1:T(8,128)(2,1)}) %reduce-scatter.15.cloned.1.call-update) | async-done | bytes 131088 | tf_op jit(solution)/shard_map/reduce_scatter | solution.py:25
  66.3 0.0 reduce-scatter.19.cloned.1.call-update
  66.4 0.0 reduce-scatter.17.cloned.1.call-start
  66.4 0.1 copy.25
  66.5 24.9 %reduce-scatter.19.cloned.1.call-done = bf16[1,1,128,128]{2,3,0,1:T(8,128)(2,1)} async-done(((bf16[4,1,128,128]{2,3,0,1:T(8,128)(2,1)}), bf16[1,1,128,128]{2,3,0,1:T(8,128)(2,1)}) %reduce-scatter.19.cloned.1.call-update) | async-done | bytes 32784
  91.4 0.8 convert_subtract_fusion.1
  92.2 10.0 %all-gather.1 = f32[1,1,512,128]{2,3,0,1:T(8,128)S(1)} all-gather(f32[1,1,128,128]{2,3,0,1:T(8,128)S(1)} %convert_subtract_fusion.1), channel_id=3, replica_groups=mesh['prow'=4,'pcol'=8] {'prow'}, dimensions={2}, use_global_device_ids=true | all-gather | bytes 327680 | tf_op jit(solution)/shard_map/all_gather | solution.py:32
  102.2 0.0 copy-done.1
  102.2 0.7 convolution_convert_fusion
  102.9 2.6 %fusion.4 = f32[2,4,8,128,128]{3,4,1,2,0:T(8,128)} fusion(f32[2,4,8,128,128]{3,4,1,2,0:T(8,128)} %copy-done, s32[]{:T(128)} %bitcast.16, s32[]{:T(128)} %bitcast.17, bf16[4,128,512]{2,1,0:T(8,128)(2,1)S(1)} %bitcast.81, bf16[128,512]{1,0:T(8,128)(2,1)S(1)} %convolution_convert_fusion, pred[]{:T(512)} %get-tuple-element.29), kind=kOutput, calls=%fused_computation.8 | convolution fusion | flops 67239936 | bytes 1181184 | tf_op jit(solution)/shard_map/wsiq,wqm->wsim/dot_general | solution.py:44
  105.5 2.7 %fusion.6 = bf16[4,8,128,128]{2,3,0,1:T(8,128)(2,1)} fusion(f32[2,4,8,128,128]{3,4,1,2,0:T(8,128)} %fusion.4), kind=kLoop, calls=%fused_computation.12 | loop fusion | bytes 2097152 | tf_op jit(solution)/shard_map/convert_element_type | solution.py:26
  108.2 0.0 reduce-scatter.17.cloned.1.call-update
  108.2 0.0 reduce-scatter.21.cloned.1.call-start
  108.2 32.7 %reduce-scatter.17.cloned.1.call-done = bf16[4,1,128,128]{2,3,0,1:T(8,128)(2,1)} async-done(((bf16[4,8,128,128]{2,3,0,1:T(8,128)(2,1)}), bf16[4,1,128,128]{2,3,0,1:T(8,128)(2,1)}) %reduce-scatter.17.cloned.1.call-update) | async-done | bytes 131088 | tf_op jit(solution)/shard_map/reduce_scatter | solution.py:25
  140.9 0.0 reduce-scatter.21.cloned.1.call-update
  141.0 0.1 copy.26
  141.1 0.1 copy.17
  141.2 24.6 %reduce-scatter.21.cloned.1.call-done = bf16[1,1,128,128]{2,3,0,1:T(8,128)(2,1)} async-done(((bf16[4,1,128,128]{2,3,0,1:T(8,128)(2,1)}), bf16[1,1,128,128]{2,3,0,1:T(8,128)(2,1)}) %reduce-scatter.21.cloned.1.call-update) | async-done | bytes 32784
  165.9 0.8 convert_subtract_fusion
  166.7 10.0 %all-gather.2 = f32[1,1,512,128]{2,3,0,1:T(8,128)S(1)} all-gather(f32[1,1,128,128]{2,3,0,1:T(8,128)S(1)} %convert_subtract_fusion), channel_id=4, replica_groups=mesh['prow'=4,'pcol'=8] {'prow'}, dimensions={2}, use_global_device_ids=true | all-gather | bytes 327680 | tf_op jit(solution)/shard_map/all_gather | solution.py:32
  176.7 0.7 fusion.7
  177.4 0.8 copy.18
  (4 shorter events, 0.1 us)
Async XLA Ops:
  6.5 59.8 %reduce-scatter.15.cloned.1.call-start = ((), (), s32[]{:S(2)}) async-start(), calls=%async_computation.4 | async-start | bytes 1179648 | tf_op jit(solution)/shard_map/reduce_scatter | solution.py:25
  28.7 73.4 %copy-start.1 = (bf16[3,1,512,512]{3,2,1,0:T(8,128)(2,1)S(1)}, bf16[3,1,512,512]{3,2,1,0:T(8,128)(2,1)}, u32[]{:S(2)}) copy-start(bf16[3,1,512,512]{3,2,1,0:T(8,128)(2,1)} %param.9) | copy-start | bytes 4718596
  30.2 1.9 %copy-start = (f32[2,4,8,128,128]{3,4,1,2,0:T(8,128)}, f32[2,4,8,128,128]{3,4,1,2,0:T(8,128)S(1)}, u32[]{:S(2)}) copy-start(f32[2,4,8,128,128]{3,4,1,2,0:T(8,128)S(1)} %fusion.1) | copy-start | bytes 12582916
  33.3 58.1 %reduce-scatter.19.cloned.1.call-start = ((), (), s32[]{:S(2)}) async-start(), calls=%async_computation.6 | async-start | bytes 163840
  66.4 74.6 %reduce-scatter.17.cloned.1.call-start = ((), (), s32[]{:S(2)}) async-start(), calls=%async_computation.5 | async-start | bytes 1179648 | tf_op jit(solution)/shard_map/reduce_scatter | solution.py:25
  108.2 57.7 %reduce-scatter.21.cloned.1.call-start = ((), (), s32[]{:S(2)}) async-start(), calls=%async_computation.7 | async-start | bytes 163840
Sparse Core Ops, SparseCore 0:
  33.4 32.8 reduce-scatter.14
  69.1 22.3 reduce-scatter.18
  108.3 32.5 reduce-scatter.16
  143.5 22.3 reduce-scatter.20
where the time goes:
time: 185 us
  waiting for transfers between devices  115 us (62%)
  blocking collectives  30.4 us (16%)
  between operations  18.4 us (10%)
  local copies, waits for them, and re-layouts  10.1 us (5%)
  matrix products  6.49 us (4%)
  other arithmetic  3.72 us (2%)
    reduce_scatter x2, waiting for transfers between devices, local(): lax.psum_scatter(due_block.astype(jnp.bfloat16), 'pcol', scatter_dimensio...  65.7 us
    unnamed x6, waiting for transfers between devices  49.6 us
    all_gather x3, blocking collectives, local(): whole_block = lax.all_gather(remaining_rhs, 'prow', axis=1, tiled=True)  30.4 us
    convert_element_type x2, local copies, waits for them, and re-layouts, local(): due_block.astype(jnp.bfloat16)  3.85 us
  transfers between devices with their start and end apart: 4, of which 4 were waited for; matrix products, arithmetic and copies ran while one was open for 0% of the time, Pallas kernels for 0%

commit v1 on v0

--- a/solution.py
+++ b/solution.py
@@ -2,6 +2,18 @@
 import jax.numpy as jnp
 from jax import lax
 from jax.sharding import PartitionSpec as P
+
+
+def tell_floor(target, link_axis, dim_i):
+    nd = lax.axis_size(link_axis)
+    u = 1
+    vals = [target]
+    while u < nd:
+        main = lax.ppermute(vals[u - 1], link_axis, [(rr, (rr - 1) % nd) for rr in range(nd)])
+        vals.append(main)
+        u = u + 1
+    current_value = jnp.concatenate(vals, axis=dim_i)
+    return jnp.roll(current_value, lax.axis_index(link_axis) * target.shape[dim_i], axis=dim_i)
 
 
 def local(rhs, inverse_diagonal_blocks, offdiagonal_blocks, targets):
@@ -29,7 +41,7 @@
                 reduced_once, "prow", scatter_dimension=0, tiled=True
             ).astype(jnp.float32)[0]
             remaining_rhs = remaining_rhs - arrived
-        whole_block = lax.all_gather(remaining_rhs, "prow", axis=1, tiled=True)
+        whole_block = tell_floor(remaining_rhs, "prow", 1)
         finished_unknowns = jnp.einsum(
             "rqe,rei->rqi",
             inverse_diagonal_blocks[present_level].astype(jnp.float32),

time: 185 us -> 195 us (1.054)
  blocking collectives: 30.4 us -> 0 us
  starting transfers between devices: 0.12 us -> 21 us
  waiting for transfers between devices: 115 us -> 135 us
    all_gather x3 -> x0, blocking collectives: 30.4 us -> none  [local(): whole_block = lax.all_gather(remaining_rhs, 'prow', axis=1, tiled=True)]
    ppermute x0 -> x9, starting transfers between devices: none -> 20.8 us  [tell_floor(): lax.ppermute(vals[u - 1], link_axis, [(rr, (rr - 1) % nd) for rr in range...]
    ppermute x0 -> x9, waiting for transfers between devices: none -> 18.1 us  [tell_floor(): lax.ppermute(vals[u - 1], link_axis, [(rr, (rr - 1) % nd) for rr in range...]
  transfers between devices with their start and end apart: 4 -> 13, of which waited for: 4 -> 12; matrix products, arithmetic and copies ran while one was open for 0% -> 2% of each run, Pallas kernels for 0% -> 0%
where the time goes in v1:
time: 195 us
  waiting for transfers between devices  135 us (69%)
  starting transfers between devices  21 us (11%)
  between operations  18.4 us (9%)
  local copies, waits for them, and re-layouts  10 us (5%)
  matrix products  6.93 us (4%)
  other arithmetic  3.71 us (2%)
    reduce_scatter x2, waiting for transfers between devices, local(): lax.psum_scatter(due_block.astype(jnp.bfloat16), 'pcol', scatter_dimensio...  66.6 us
    unnamed x6, waiting for transfers between devices  49.8 us
    ppermute x9, starting transfers between devices, tell_floor(): lax.ppermute(vals[u - 1], link_axis, [(rr, (rr - 1) % nd) for rr in range...  20.8 us
    ppermute x9, waiting for transfers between devices, tell_floor(): lax.ppermute(vals[u - 1], link_axis, [(rr, (rr - 1) % nd) for rr in range...  18.1 us
  transfers between devices with their start and end apart: 13, of which 12 were waited for; matrix products, arithmetic and copies ran while one was open for 2% of the time, Pallas kernels for 0%

profile of v1, /device:TPU:0, one launch (start us, length us, event | category | flops | bytes accessed | tf_op | source)
XLA Modules:
  0.0 194.6 jit_solution(10775570923343016875)
XLA Ops:
  6.5 0.8 fusion.54
  7.3 4.0 %collective-permute-start = (f32[1,128,128]{2,1,0:T(8,128)S(1)}, f32[1,128,128]{2,1,0:T(8,128)S(1)}, u32[]{:S(2)}, u32[]{:S(2)}) collective-permute-start(f32[1,128,128]{2,1,0:T(8,128)S(1)} %get-tuple-element.36), channel_id=1, source_target_pairs={{0,24},{8,0},{16,8},{24,16},{1,25},{9,1},{17,9},{25,17},{2,26},{10... | collective-permute-start | bytes 196616 | tf_op jit(solution)/shard_map/ppermute | solution.py:12
  11.3 1.3 fusion.53
  12.6 0.6 collective-permute-done
  13.2 3.3 %collective-permute-start.1 = (f32[1,128,128]{2,1,0:T(8,128)S(1)}, f32[1,128,128]{2,1,0:T(8,128)S(1)}, u32[]{:S(2)}, u32[]{:S(2)}) collective-permute-start(f32[1,128,128]{2,1,0:T(8,128)S(1)} %collective-permute-done), channel_id=1, source_target_pairs={{0,24},{8,0},{16,8},{24,16},{1,25},{9,1},{17,9},{25,17},{2,26},{10... | collective-permute-start | bytes 196616 | tf_op jit(solution)/shard_map/ppermute | solution.py:12
  16.5 0.7 fusion.55
  17.2 0.6 constant_dynamic-slice_fusion
  23.0 0.1 concatenate.23
  23.1 0.1 concatenate.25
  23.1 1.4 and_reduce_fusion
  24.5 2.9 %collective-permute-done.2 = f32[1,128,128]{2,1,0:T(8,128)S(1)} collective-permute-done((f32[1,128,128]{2,1,0:T(8,128)S(1)}, f32[1,128,128]{2,1,0:T(8,128)S(1)}, u32[]{:S(2)}, u32[]{:S(2)}) %collective-permute-start.2) | collective-permute-done | bytes 65568 | tf_op jit(solution)/shard_map/ppermute | solution.py:12
  27.4 2.2 %convolution_convert_fusion.1 = bf16[128,512]{1,0:T(8,128)(2,1)S(1)} fusion(bf16[3,1,512,512]{3,2,1,0:T(8,128)(2,1)} %param.11, s32[]{:T(128)S(6)} %select_n.64, f32[1,128,128]{2,1,0:T(8,128)S(1)} %get-tuple-element.36, f32[1,128,128]{2,1,0:T(8,128)S(1)} %collective-permute-done, f32[1,128,128]{2,1,0:T(8,128)S(1)} %collective-permute-done.1, ...), kind=kOutput, calls=%fused_computation.10 | convolution fusion | flops 403177472 | bytes 917508 | tf_op jit(solution)/shard_map/rqe,rei->rqi/dot_general | solution.py:45
  29.6 0.5 broadcast_in_dim.2
  30.1 0.9 fusion.1
  31.1 1.9 copy-done
  33.0 1.1 fusion.5
  34.2 0.0 reduce-scatter.15.cloned.1.call-update
  34.2 0.0 reduce-scatter.19.cloned.1.call-start
  34.2 32.4 %reduce-scatter.15.cloned.1.call-done = bf16[4,1,128,128]{2,3,0,1:T(8,128)(2,1)} async-done(((bf16[4,8,128,128]{2,3,0,1:T(8,128)(2,1)}), bf16[4,1,128,128]{2,3,0,1:T(8,128)(2,1)}) %reduce-scatter.15.cloned.1.call-update) | async-done | bytes 131088 | tf_op jit(solution)/shard_map/reduce_scatter | solution.py:37
  66.6 0.0 reduce-scatter.19.cloned.1.call-update
  66.7 0.0 reduce-scatter.17.cloned.1.call-start
  66.7 0.1 copy.15
  66.8 24.9 %reduce-scatter.19.cloned.1.call-done = bf16[1,1,128,128]{2,3,0,1:T(8,128)(2,1)} async-done(((bf16[4,1,128,128]{2,3,0,1:T(8,128)(2,1)}), bf16[1,1,128,128]{2,3,0,1:T(8,128)(2,1)}) %reduce-scatter.19.cloned.1.call-update) | async-done | bytes 32784
  91.8 0.8 subtract_bitcast_fusion.1
  92.5 1.5 collective-permute-start.3
  94.0 2.8 %collective-permute-done.3 = f32[1,128,128]{1,2,0:T(8,128)S(1)} collective-permute-done((f32[1,128,128]{1,2,0:T(8,128)S(1)}, f32[1,128,128]{1,2,0:T(8,128)S(1)}, u32[]{:S(2)}, u32[]{:S(2)}) %collective-permute-start.3) | collective-permute-done | bytes 65568 | tf_op jit(solution)/shard_map/ppermute | solution.py:12
  96.9 2.4 %collective-permute-start.4 = (f32[1,128,128]{1,2,0:T(8,128)S(1)}, f32[1,128,128]{1,2,0:T(8,128)S(1)}, u32[]{:S(2)}, u32[]{:S(2)}) collective-permute-start(f32[1,128,128]{1,2,0:T(8,128)S(1)} %collective-permute-done.3), channel_id=1, source_target_pairs={{0,24},{8,0},{16,8},{24,16},{1,25},{9,1},{17,9},{25,17},{2,26},{10... | collective-permute-start | bytes 196616 | tf_op jit(solution)/shard_map/ppermute | solution.py:12
  99.2 2.2 %collective-permute-done.4 = f32[1,128,128]{1,2,0:T(8,128)S(1)} collective-permute-done((f32[1,128,128]{1,2,0:T(8,128)S(1)}, f32[1,128,128]{1,2,0:T(8,128)S(1)}, u32[]{:S(2)}, u32[]{:S(2)}) %collective-permute-start.4) | collective-permute-done | bytes 65568 | tf_op jit(solution)/shard_map/ppermute | solution.py:12
  101.5 2.9 %collective-permute-start.5 = (f32[1,128,128]{1,2,0:T(8,128)S(1)}, f32[1,128,128]{1,2,0:T(8,128)S(1)}, u32[]{:S(2)}, u32[]{:S(2)}) collective-permute-start(f32[1,128,128]{1,2,0:T(8,128)S(1)} %collective-permute-done.4), channel_id=1, source_target_pairs={{0,24},{8,0},{16,8},{24,16},{1,25},{9,1},{17,9},{25,17},{2,26},{10... | collective-permute-start | bytes 196616 | tf_op jit(solution)/shard_map/ppermute | solution.py:12
  104.4 2.2 %collective-permute-done.5 = f32[1,128,128]{1,2,0:T(8,128)S(1)} collective-permute-done((f32[1,128,128]{1,2,0:T(8,128)S(1)}, f32[1,128,128]{1,2,0:T(8,128)S(1)}, u32[]{:S(2)}, u32[]{:S(2)}) %collective-permute-start.5) | collective-permute-done | bytes 65568 | tf_op jit(solution)/shard_map/ppermute | solution.py:12
  106.6 0.6 convolution_convert_fusion
  107.3 2.5 %fusion.4 = f32[2,4,8,128,128]{3,4,1,2,0:T(8,128)} fusion(f32[2,4,8,128,128]{3,4,1,2,0:T(8,128)} %copy-done, s32[]{:T(128)} %bitcast.20, s32[]{:T(128)} %bitcast.21, bf16[4,128,512]{2,1,0:T(8,128)(2,1)S(1)} %bitcast.90, bf16[128,512]{1,0:T(8,128)(2,1)S(1)} %convolution_convert_fusion, pred[]{:T(512)} %get-tuple-element.30), kind=kOutput, calls=%fused_computation.8 | convolution fusion | flops 67239936 | bytes 1181184 | tf_op jit(solution)/shard_map/wsiq,wqm->wsim/dot_general | solution.py:56
  109.8 2.7 %fusion.6 = bf16[4,8,128,128]{2,3,0,1:T(8,128)(2,1)} fusion(f32[2,4,8,128,128]{3,4,1,2,0:T(8,128)} %fusion.4), kind=kLoop, calls=%fused_computation.12 | loop fusion | bytes 2097152 | tf_op jit(solution)/shard_map/convert_element_type | solution.py:38
  112.5 0.0 reduce-scatter.17.cloned.1.call-update
  112.5 0.0 reduce-scatter.21.cloned.1.call-start
  112.6 34.2 %reduce-scatter.17.cloned.1.call-done = bf16[4,1,128,128]{2,3,0,1:T(8,128)(2,1)} async-done(((bf16[4,8,128,128]{2,3,0,1:T(8,128)(2,1)}), bf16[4,1,128,128]{2,3,0,1:T(8,128)(2,1)}) %reduce-scatter.17.cloned.1.call-update) | async-done | bytes 131088 | tf_op jit(solution)/shard_map/reduce_scatter | solution.py:37
  146.8 0.0 reduce-scatter.21.cloned.1.call-update
  146.8 0.1 copy.16
  146.9 24.8 %reduce-scatter.21.cloned.1.call-done = bf16[1,1,128,128]{2,3,0,1:T(8,128)(2,1)} async-done(((bf16[4,1,128,128]{2,3,0,1:T(8,128)(2,1)}), bf16[1,1,128,128]{2,3,0,1:T(8,128)(2,1)}) %reduce-scatter.21.cloned.1.call-update) | async-done | bytes 32784
  171.7 0.8 subtract_bitcast_fusion
  172.5 1.5 collective-permute-start.6
  174.0 2.8 %collective-permute-done.6 = f32[1,128,128]{1,2,0:T(8,128)S(1)} collective-permute-done((f32[1,128,128]{1,2,0:T(8,128)S(1)}, f32[1,128,128]{1,2,0:T(8,128)S(1)}, u32[]{:S(2)}, u32[]{:S(2)}) %collective-permute-start.6) | collective-permute-done | bytes 65568 | tf_op jit(solution)/shard_map/ppermute | solution.py:12
  176.8 2.4 %collective-permute-start.7 = (f32[1,128,128]{1,2,0:T(8,128)S(1)}, f32[1,128,128]{1,2,0:T(8,128)S(1)}, u32[]{:S(2)}, u32[]{:S(2)}) collective-permute-start(f32[1,128,128]{1,2,0:T(8,128)S(1)} %collective-permute-done.6), channel_id=1, source_target_pairs={{0,24},{8,0},{16,8},{24,16},{1,25},{9,1},{17,9},{25,17},{2,26},{10... | collective-permute-start | bytes 196616 | tf_op jit(solution)/shard_map/ppermute | solution.py:12
  179.2 2.2 %collective-permute-done.7 = f32[1,128,128]{1,2,0:T(8,128)S(1)} collective-permute-done((f32[1,128,128]{1,2,0:T(8,128)S(1)}, f32[1,128,128]{1,2,0:T(8,128)S(1)}, u32[]{:S(2)}, u32[]{:S(2)}) %collective-permute-start.7) | collective-permute-done | bytes 65568 | tf_op jit(solution)/shard_map/ppermute | solution.py:12
  181.4 2.9 %collective-permute-start.8 = (f32[1,128,128]{1,2,0:T(8,128)S(1)}, f32[1,128,128]{1,2,0:T(8,128)S(1)}, u32[]{:S(2)}, u32[]{:S(2)}) collective-permute-start(f32[1,128,128]{1,2,0:T(8,128)S(1)} %collective-permute-done.7), channel_id=1, source_target_pairs={{0,24},{8,0},{16,8},{24,16},{1,25},{9,1},{17,9},{25,17},{2,26},{10... | collective-permute-start | bytes 196616 | tf_op jit(solution)/shard_map/ppermute | solution.py:12
  184.4 2.2 %collective-permute-done.8 = f32[1,128,128]{1,2,0:T(8,128)S(1)} collective-permute-done((f32[1,128,128]{1,2,0:T(8,128)S(1)}, f32[1,128,128]{1,2,0:T(8,128)S(1)}, u32[]{:S(2)}, u32[]{:S(2)}) %collective-permute-start.8) | collective-permute-done | bytes 65568 | tf_op jit(solution)/shard_map/ppermute | solution.py:12
  186.6 0.6 fusion.7
  187.3 0.8 copy.10
  (10 shorter events, 0.1 us)
Async XLA Ops:
  6.5 60.1 %reduce-scatter.15.cloned.1.call-start = ((), (), s32[]{:S(2)}) async-start(), calls=%async_computation.4 | async-start | bytes 1179648 | tf_op jit(solution)/shard_map/reduce_scatter | solution.py:37
  7.3 5.9 %collective-permute-start = (f32[1,128,128]{2,1,0:T(8,128)S(1)}, f32[1,128,128]{2,1,0:T(8,128)S(1)}, u32[]{:S(2)}, u32[]{:S(2)}) collective-permute-start(f32[1,128,128]{2,1,0:T(8,128)S(1)} %get-tuple-element.36), channel_id=1, source_target_pairs={{0,24},{8,0},{16,8},{24,16},{1,25},{9,1},{17,9},{25,17},{2,26},{10... | collective-permute-start | bytes 196616 | tf_op jit(solution)/shard_map/ppermute | solution.py:12
  13.2 9.9 %collective-permute-start.1 = (f32[1,128,128]{2,1,0:T(8,128)S(1)}, f32[1,128,128]{2,1,0:T(8,128)S(1)}, u32[]{:S(2)}, u32[]{:S(2)}) collective-permute-start(f32[1,128,128]{2,1,0:T(8,128)S(1)} %collective-permute-done), channel_id=1, source_target_pairs={{0,24},{8,0},{16,8},{24,16},{1,25},{9,1},{17,9},{25,17},{2,26},{10... | collective-permute-start | bytes 196616 | tf_op jit(solution)/shard_map/ppermute | solution.py:12
  23.1 4.3 %collective-permute-start.2 = (f32[1,128,128]{2,1,0:T(8,128)S(1)}, f32[1,128,128]{2,1,0:T(8,128)S(1)}, u32[]{:S(2)}, u32[]{:S(2)}) collective-permute-start(f32[1,128,128]{2,1,0:T(8,128)S(1)} %collective-permute-done.1), channel_id=1, source_target_pairs={{0,24},{8,0},{16,8},{24,16},{1,25},{9,1},{17,9},{25,17},{2,26},{10... | collective-permute-start | bytes 196616 | tf_op jit(solution)/shard_map/ppermute | solution.py:12
  29.6 77.0 %copy-start.1 = (bf16[3,1,512,512]{3,2,1,0:T(8,128)(2,1)S(1)}, bf16[3,1,512,512]{3,2,1,0:T(8,128)(2,1)}, u32[]{:S(2)}) copy-start(bf16[3,1,512,512]{3,2,1,0:T(8,128)(2,1)} %param.11) | copy-start | bytes 4718596
  31.1 1.9 %copy-start = (f32[2,4,8,128,128]{3,4,1,2,0:T(8,128)}, f32[2,4,8,128,128]{3,4,1,2,0:T(8,128)S(1)}, u32[]{:S(2)}) copy-start(f32[2,4,8,128,128]{3,4,1,2,0:T(8,128)S(1)} %fusion.1) | copy-start | bytes 12582916
  34.2 57.6 %reduce-scatter.19.cloned.1.call-start = ((), (), s32[]{:S(2)}) async-start(), calls=%async_computation.6 | async-start | bytes 163840
  66.7 80.1 %reduce-scatter.17.cloned.1.call-start = ((), (), s32[]{:S(2)}) async-start(), calls=%async_computation.5 | async-start | bytes 1179648 | tf_op jit(solution)/shard_map/reduce_scatter | solution.py:37
  92.5 4.3 %collective-permute-start.3 = (f32[1,128,128]{1,2,0:T(8,128)S(1)}, f32[1,128,128]{1,2,0:T(8,128)S(1)}, u32[]{:S(2)}, u32[]{:S(2)}) collective-permute-start(f32[1,128,128]{1,2,0:T(8,128)S(1)} %subtract_bitcast_fusion.1), channel_id=1, source_target_pairs={{0,24},{8,0},{16,8},{24,16},{1,25},{9,1},{17,9},{25,17},{2,26},{10... | collective-permute-start | bytes 196616 | tf_op jit(solution)/shard_map/ppermute | solution.py:12
  96.9 4.6 %collective-permute-start.4 = (f32[1,128,128]{1,2,0:T(8,128)S(1)}, f32[1,128,128]{1,2,0:T(8,128)S(1)}, u32[]{:S(2)}, u32[]{:S(2)}) collective-permute-start(f32[1,128,128]{1,2,0:T(8,128)S(1)} %collective-permute-done.3), channel_id=1, source_target_pairs={{0,24},{8,0},{16,8},{24,16},{1,25},{9,1},{17,9},{25,17},{2,26},{10... | collective-permute-start | bytes 196616 | tf_op jit(solution)/shard_map/ppermute | solution.py:12
  101.5 5.2 %collective-permute-start.5 = (f32[1,128,128]{1,2,0:T(8,128)S(1)}, f32[1,128,128]{1,2,0:T(8,128)S(1)}, u32[]{:S(2)}, u32[]{:S(2)}) collective-permute-start(f32[1,128,128]{1,2,0:T(8,128)S(1)} %collective-permute-done.4), channel_id=1, source_target_pairs={{0,24},{8,0},{16,8},{24,16},{1,25},{9,1},{17,9},{25,17},{2,26},{10... | collective-permute-start | bytes 196616 | tf_op jit(solution)/shard_map/ppermute | solution.py:12
  112.5 59.2 %reduce-scatter.21.cloned.1.call-start = ((), (), s32[]{:S(2)}) async-start(), calls=%async_computation.7 | async-start | bytes 163840
  172.5 4.3 %collective-permute-start.6 = (f32[1,128,128]{1,2,0:T(8,128)S(1)}, f32[1,128,128]{1,2,0:T(8,128)S(1)}, u32[]{:S(2)}, u32[]{:S(2)}) collective-permute-start(f32[1,128,128]{1,2,0:T(8,128)S(1)} %subtract_bitcast_fusion), channel_id=1, source_target_pairs={{0,24},{8,0},{16,8},{24,16},{1,25},{9,1},{17,9},{25,17},{2,26},{10... | collective-permute-start | bytes 196616 | tf_op jit(solution)/shard_map/ppermute | solution.py:12
  176.8 4.6 %collective-permute-start.7 = (f32[1,128,128]{1,2,0:T(8,128)S(1)}, f32[1,128,128]{1,2,0:T(8,128)S(1)}, u32[]{:S(2)}, u32[]{:S(2)}) collective-permute-start(f32[1,128,128]{1,2,0:T(8,128)S(1)} %collective-permute-done.6), channel_id=1, source_target_pairs={{0,24},{8,0},{16,8},{24,16},{1,25},{9,1},{17,9},{25,17},{2,26},{10... | collective-permute-start | bytes 196616 | tf_op jit(solution)/shard_map/ppermute | solution.py:12
  181.4 5.2 %collective-permute-start.8 = (f32[1,128,128]{1,2,0:T(8,128)S(1)}, f32[1,128,128]{1,2,0:T(8,128)S(1)}, u32[]{:S(2)}, u32[]{:S(2)}) collective-permute-start(f32[1,128,128]{1,2,0:T(8,128)S(1)} %collective-permute-done.7), channel_id=1, source_target_pairs={{0,24},{8,0},{16,8},{24,16},{1,25},{9,1},{17,9},{25,17},{2,26},{10... | collective-permute-start | bytes 196616 | tf_op jit(solution)/shard_map/ppermute | solution.py:12
Sparse Core Ops, SparseCore 0:
  34.3 32.3 reduce-scatter.14
  69.4 22.3 reduce-scatter.18
  112.6 34.0 reduce-scatter.16
  149.4 22.3 reduce-scatter.20
